TPU v7x, 256 devices: a whole 4x4x8 slice. The times are simulated.
256 devices in a mesh: row: 16 (over x, z_lo), col: 16 (over y, z_hi, core).
Axes of the slice: x: 4, y: 4, z: 8 (z_hi: 2, z_lo: 4; z = z_hi * 4 + z_lo), core: 2. Of those that a mesh axis runs over, the one named last changes fastest.
Arguments:
- potential: float32 [32, 64, 512], P('row', 'col'), may hold values from -6 to 6
- basis: bfloat16 [32, 64, 384, 512], P('row', 'col'), may hold values from -6 to 6
- hamiltonian: bfloat16 [6144, 6144], P('row', 'col'), may hold values from -0.078125 to 0.078125
- density: bfloat16 [2, 6144, 6144], P(None, 'row', 'col'), may hold values from -6 to 6
- hmask: int32 [48, 48], replicated, may hold values from 0 to 1, as said below
- pmask: int32 [48, 48], replicated, may hold values from 0 to 1, as said below
Outputs:
- propagated: bfloat16 [2, 6144, 6144], P(None, 'row', 'col')
Inputs may be any that keep to these rules, and one draw needn't show every extreme that they name: hmask[I, I] is always 1; every other block is 1 with probability 1/2, independently. pmask follows the same law as hmask, drawn independently.
All inputs are finite; a program needn't handle non-finite values.
Results may differ from a plain program's by a relative error of at most 0.0062.
Values may be sent and summed in bfloat16 or wider, within the bound.
A program may use at most 64 MiB of HBM per device.

v0:
```python
import jax
import jax.numpy as jnp
from jax import lax
from jax.sharding import PartitionSpec as P

BLK = 128
KAPPA = 0.4
TIME_STEP = 0.5


def extended_2(block, sides, width):
    for axis, dim in sides:
        count = lax.axis_size(axis)
        forward = [(i, i + 1) for i in range(count - 1)]
        backward = [(target, source) for source, target in forward]
        low = lax.ppermute(
            lax.slice_in_dim(block, block.shape[dim] - width, None, axis=dim), axis, forward
        )
        high = lax.ppermute(lax.slice_in_dim(block, 0, width, axis=dim), axis, backward)
        block = jnp.concatenate([low, block, high], axis=dim)
    return block


def shards(potential, basis, hamiltonian, density, hmask, pmask):
    width_x, width_y, depth_z = potential.shape
    extended = extended_2(potential, (("row", 0), ("col", 1)), 1)
    padded = jnp.pad(extended, ((0, 0), (0, 0), (1, 1)))
    beside = padded[2:, 1:-1, 1:-1] + padded[:-2, 1:-1, 1:-1]
    beside = beside + padded[1:-1, 2:, 1:-1] + padded[1:-1, :-2, 1:-1]
    beside = beside + padded[1:-1, 1:-1, 2:] + padded[1:-1, 1:-1, :-2]
    effective = potential + KAPPA * (beside - 6.0 * potential)
    blocks_here = basis.shape[2] // BLK
    weighted = (basis * effective[:, :, None, :]).astype(jnp.bfloat16)
    partial_blocks = jnp.einsum(
        "xykaz,xykbz->kab",
        weighted.reshape(width_x, width_y, blocks_here, BLK, depth_z),
        basis.reshape(width_x, width_y, blocks_here, BLK, depth_z),
        preferred_element_type=jnp.float32,
    )
    summed = lax.psum(partial_blocks, "col")
    factor = float(BLK * width_x * width_y * depth_z * lax.axis_size("col")) ** (-0.5)
    potential_blocks = (summed * factor).astype(jnp.bfloat16)
    block_total = hmask.shape[0]
    blocks_wide = block_total // lax.axis_size("col")
    row_start = lax.axis_index("row") * blocks_here
    col_start = lax.axis_index("col") * blocks_wide
    hpattern = lax.dynamic_slice(hmask, (row_start, col_start), (blocks_here, blocks_wide))
    ppattern = lax.dynamic_slice(pmask, (row_start, col_start), (blocks_here, blocks_wide))
    masked_h = (
        hamiltonian.reshape(blocks_here, BLK, blocks_wide, BLK)
        * hpattern[:, None, :, None].astype(jnp.bfloat16)
    ).reshape(blocks_here * BLK, blocks_wide * BLK)
    masked_p = (
        density.reshape(2, blocks_here, BLK, blocks_wide, BLK)
        * ppattern[None, :, None, :, None].astype(jnp.bfloat16)
    ).reshape(2, blocks_here * BLK, blocks_wide * BLK)

    def diagonal_term(operand):
        local = jnp.einsum(
            "kab,skbc->skac",
            potential_blocks,
            operand.reshape(2, blocks_here, BLK, operand.shape[2]),
            preferred_element_type=jnp.float32,
        )
        return local.reshape(2, blocks_here * BLK, operand.shape[2])

    def apply(operand):
        column_whole = lax.all_gather(operand, "row", axis=1, tiled=True)
        remote = jnp.einsum(
            "rk,skc->src",
            lax.all_gather(masked_h, "col", axis=1, tiled=True),
            column_whole,
            preferred_element_type=jnp.float32,
        )
        return remote + diagonal_term(operand)

    first = apply(masked_p)
    first_rounded = first.astype(jnp.bfloat16)
    second = apply(first_rounded)
    base = masked_p.astype(jnp.float32)
    half_square = 0.5 * TIME_STEP * TIME_STEP
    real_part = base[0] + TIME_STEP * first[1] - half_square * second[0]
    imag_part = base[1] - TIME_STEP * first[0] - half_square * second[1]
    stacked = jnp.stack([real_part, imag_part]).reshape(2, blocks_here, BLK, blocks_wide, BLK)
    stacked = stacked * ppattern[None, :, None, :, None].astype(jnp.float32)
    return stacked.reshape(2, blocks_here * BLK, blocks_wide * BLK).astype(jnp.bfloat16)


def solution(mesh):
    in_specs = (
        P("row", "col", None),
        P("row", "col", None, None),
        P("row", "col"),
        P(None, "row", "col"),
        P(),
        P(),
    )
    out_specs = P(None, "row", "col")
    return jax.shard_map(shards, mesh=mesh, in_specs=in_specs, out_specs=out_specs, check_vma=False)
```

profile of v0, /device:TPU:1, one launch (start us, length us, event | category | flops | bytes accessed | tf_op | source)
XLA Modules:
  0.0 729.8 jit_solution(5748484860902074060)
XLA Ops:
  6.5 0.0 all-reduce.3.cloned.1.call-start
  6.5 0.7 fusion.37
  7.3 4.3 collective-permute-start.1
  11.6 1.3 collective-permute-start
  12.9 0.0 collective-permute-done.1
  12.9 0.7 constant_dynamic-update-slice_fusion.1
  13.7 2.5 collective-permute-done
  16.2 3.8 collective-permute-start.2
  20.1 7.8 %collective-permute-start.3 = (f32[4,1,512]{2,1,0:T(1,128)S(1)}, f32[4,1,512]{2,1,0:T(1,128)S(1)}, u32[]{:S(2)}, u32[]{:S(2)}) collective-permute-start(f32[4,1,512]{2,1,0:T(1,128)S(1)} %get-tuple-element.9), channel_id=1, source_target_pairs={{0,1},{1,2},{2,3},{3,4},{4,5},{5,6},{6,7},{7,8},{8,9},{9,10},{10,1... | collective-permute-start | bytes 24584 | tf_op jit(solution)/shard_map/ppermute | solution.py:16
  27.9 0.8 dynamic-slice_convert_fusion.1
  28.7 0.0 collective-permute-done.2
  28.7 0.0 collective-permute-done.3
  28.7 0.1 select_maximum_fusion
  28.8 0.9 fusion.29
  29.7 0.0 copy-start
  29.7 2.7 multiply_convert_fusion
  32.5 0.1 copy-done
  32.6 1.7 convolution_bitcast_fusion.2
  34.2 0.0 all-reduce.3.cloned.1.call-update
  34.2 0.0 all-gather.6.cloned.1.call-start
  34.3 0.2 mul.100
  34.5 0.0 copy-done.5
  34.5 0.8 bitcast_multiply_fusion
  35.3 0.0 all-gather.6.cloned.1.call-update
  35.3 0.0 all-gather.4.cloned.1.call-start
  35.3 0.2 mul.96
  35.6 0.0 copy-done.2
  35.6 0.9 fusion.35
  36.5 0.0 all-gather.4.cloned.1.call-update
  36.6 0.0 all-gather.8.cloned.1.call-start
  36.6 0.1 broadcast_bitcast_fusion
  36.7 175.1 %all-reduce.3.cloned.1.call-done = f32[3,128,128]{2,1,0:T(8,128)} async-done(((f32[3,128,128]{2,1,0:T(8,128)}), f32[3,128,128]{2,1,0:T(8,128)}) %all-reduce.3.cloned.1.call-update) | async-done | bytes 196624 | tf_op jit(solution)/shard_map/psum | solution.py:40
  211.8 1.2 convolution_bitcast_fusion.1
  213.1 0.1 copy.18
  213.2 82.5 %all-gather.6.cloned.1.call-done = bf16[384,6144]{1,0:T(8,128)(2,1)} async-done(((bf16[384,384]{1,0:T(8,128)(2,1)}), bf16[384,6144]{1,0:T(8,128)(2,1)}) %all-gather.6.cloned.1.call-update) | async-done | bytes 4718608 | tf_op jit(solution)/shard_map/all_gather | solution.py:71
  295.7 203.1 %all-gather.4.cloned.1.call-done = bf16[2,6144,384]{2,1,0:T(8,128)(2,1)} async-done(((bf16[2,384,384]{2,1,0:T(8,128)(2,1)}), bf16[2,6144,384]{2,1,0:T(8,128)(2,1)}) %all-gather.4.cloned.1.call-update) | async-done | bytes 9437200 | tf_op jit(solution)/shard_map/all_gather | solution.py:68
  498.8 10.2 %fusion.38 = (bf16[2,384,384]{2,1,0:T(8,128)(2,1)}, f32[2,384,384]{2,1,0:T(8,128)}) fusion(f32[2,384,384]{2,1,0:T(8,128)S(1)} %bitcast.74, bf16[2,6144,384]{2,1,0:T(8,128)(2,1)} %all-gather.4.cloned.1.call-done, bf16[384,6144]{1,0:T(8,128)(2,1)} %all-gather.6.cloned.1.call-done), kind=kOutput, calls=%fused_computation.61 | convolution fusion | flops 3624468480 | bytes 17104896 | tf_op jit(solution)/shard_map/rk,skc->src/dot_general | solution.py:69
  508.9 0.0 all-gather.8.cloned.1.call-update
  509.0 0.2 mul.119
  509.1 0.1 copy.41
  509.2 0.0 copy-done.4
  509.2 0.8 copy-done.1
  510.0 0.3 convolution_bitcast_fusion
  510.3 0.1 copy.22
  510.4 203.2 %all-gather.8.cloned.1.call-done = bf16[2,6144,384]{2,1,0:T(8,128)(2,1)} async-done(((bf16[2,384,384]{2,1,0:T(8,128)(2,1)}), bf16[2,6144,384]{2,1,0:T(8,128)(2,1)}) %all-gather.8.cloned.1.call-update) | async-done | bytes 9437200 | tf_op jit(solution)/shard_map/all_gather | solution.py:68
  713.6 8.5 %fusion.13 = f32[2,384,384]{2,1,0:T(8,128)S(1)} fusion(f32[2,384,384]{2,1,0:T(8,128)S(1)} %bitcast.75, bf16[2,6144,384]{2,1,0:T(8,128)(2,1)} %all-gather.8.cloned.1.call-done, bf16[384,6144]{1,0:T(8,128)(2,1)} %all-gather.6.cloned.1.call-done), kind=kOutput, calls=%fused_computation.10 | convolution fusion | flops 3624173568 | bytes 16515072 | tf_op jit(solution)/shard_map/rk,skc->src/dot_general | solution.py:69
  722.1 0.3 fusion.19
  722.4 0.9 fusion.16
  (11 shorter events, 0.1 us)
Async XLA Ops:
  6.5 205.3 %all-reduce.3.cloned.1.call-start = ((), (), s32[]{:S(2)}) async-start(), calls=%async_computation.2 | async-start | bytes 393216 | tf_op jit(solution)/shard_map/psum | solution.py:40
  7.3 5.7 collective-permute-start.1
  11.6 4.6 collective-permute-start
  16.2 12.5 %collective-permute-start.2 = (f32[4,1,512]{2,1,0:T(1,128)S(1)}, f32[4,1,512]{2,1,0:T(1,128)S(1)}, u32[]{:S(2)}, u32[]{:S(2)}) collective-permute-start(f32[4,1,512]{2,1,0:T(1,128)S(1)} %get-tuple-element.10), channel_id=1, source_target_pairs={{1,0},{2,1},{3,2},{4,3},{5,4},{6,5},{7,6},{8,7},{9,8},{10,9},{11,1... | collective-permute-start | bytes 24584 | tf_op jit(solution)/shard_map/ppermute | solution.py:19
  20.1 8.6 %collective-permute-start.3 = (f32[4,1,512]{2,1,0:T(1,128)S(1)}, f32[4,1,512]{2,1,0:T(1,128)S(1)}, u32[]{:S(2)}, u32[]{:S(2)}) collective-permute-start(f32[4,1,512]{2,1,0:T(1,128)S(1)} %get-tuple-element.9), channel_id=1, source_target_pairs={{0,1},{1,2},{2,3},{3,4},{4,5},{5,6},{6,7},{7,8},{8,9},{9,10},{10,1... | collective-permute-start | bytes 24584 | tf_op jit(solution)/shard_map/ppermute | solution.py:16
  29.7 2.8 copy-start
  32.6 1.9 copy-start.5
  32.6 3.0 copy-start.2
  34.2 261.5 %all-gather.6.cloned.1.call-start = ((), (), s32[]{:S(2)}) async-start(), calls=%async_computation.1 | async-start | bytes 5013504 | tf_op jit(solution)/shard_map/all_gather | solution.py:71
  35.3 463.5 %all-gather.4.cloned.1.call-start = ((), (), s32[]{:S(2)}) async-start(), calls=%async_computation | async-start | bytes 10027008 | tf_op jit(solution)/shard_map/all_gather | solution.py:68
  36.6 677.0 %all-gather.8.cloned.1.call-start = ((), (), s32[]{:S(2)}) async-start(), calls=%async_computation.3 | async-start | bytes 10027008 | tf_op jit(solution)/shard_map/all_gather | solution.py:68
  498.8 10.4 %copy-start.4 = (f32[3,128,128]{2,1,0:T(8,128)S(1)}, f32[3,128,128]{2,1,0:T(8,128)}, u32[]{:S(2)}) copy-start(f32[3,128,128]{2,1,0:T(8,128)} %all-reduce.3.cloned.1.call-done) | copy-start | bytes 589828
  508.9 1.1 copy-start.1
  713.6 8.5 %copy-start.3 = (f32[2,384,384]{2,1,0:T(8,128)S(1)}, f32[2,384,384]{2,1,0:T(8,128)}, u32[]{:S(2)}) copy-start(f32[2,384,384]{2,1,0:T(8,128)} %get-tuple-element.16) | copy-start | bytes 3538948
Sparse Core Ops, SparseCore 0:
  34.4 177.4 all-reduce.2
  214.4 81.2 all-gather.5
  297.5 201.2 all-gather.3
  509.1 204.4 all-gather.7
where the time goes:
time: 730 us
  waiting for transfers between devices  667 us (91%)
  matrix products  21.9 us (3%)
  starting transfers between devices  17.4 us (2%)
  between operations  13.3 us (2%)
  other arithmetic  7.46 us (1%)
    all_gather x2, waiting for transfers between devices, apply(): column_whole = lax.all_gather(operand, 'row', axis=1, tiled=True)  406 us
    psum x1, waiting for transfers between devices, shards(): summed = lax.psum(partial_blocks, 'col')  175 us
    all_gather x1, waiting for transfers between devices, apply(): lax.all_gather(masked_h, 'col', axis=1, tiled=True)  82.5 us
    dot_general x2, matrix products, apply(): jnp.einsum('rk,skc->src', lax.all_gather(masked_h, 'col', axis=1, tiled=T...  18.7 us
  transfers between devices with their start and end apart: 8, of which 5 were waited for; matrix products, arithmetic and copies ran while one was open for 1% of the time, Pallas kernels for 0%

commit v1 on v0

--- a/solution.py
+++ b/solution.py
@@ -1,3 +1,4 @@
+import functools
 import jax
 import jax.numpy as jnp
 from jax import lax
@@ -6,6 +7,15 @@
 BLK = 128
 KAPPA = 0.4
 TIME_STEP = 0.5
+
+
+def push_the_heaps(here_x, dev_axis):
+    found_now = lax.all_gather(here_x, axis_name=dev_axis)
+    vec_out = jnp.sum(found_now, axis=0)
+    return vec_out
+
+
+node_work = functools.partial(push_the_heaps, dev_axis="col")
 
 
 def extended_2(block, sides, width):
@@ -37,7 +47,7 @@
         basis.reshape(width_x, width_y, blocks_here, BLK, depth_z),
         preferred_element_type=jnp.float32,
     )
-    summed = lax.psum(partial_blocks, "col")
+    summed = node_work(partial_blocks)
     factor = float(BLK * width_x * width_y * depth_z * lax.axis_size("col")) ** (-0.5)
     potential_blocks = (summed * factor).astype(jnp.bfloat16)
     block_total = hmask.shape[0]

time: 730 us -> 626 us (0.86)
  waiting for transfers between devices: 667 us -> 561 us
    psum x1 -> x0, waiting for transfers between devices: 175 us -> none  [shards(): summed = lax.psum(partial_blocks, 'col')]
    all_gather x0 -> x1, waiting for transfers between devices: none -> 74.1 us  [push_the_heaps(): found_now = lax.all_gather(here_x, axis_name=dev_axis)]
  transfers between devices with their start and end apart: 8 -> 8, of which waited for: 5 -> 6; matrix products, arithmetic and copies ran while one was open for 1% -> 1% of each run, Pallas kernels for 0% -> 0%
where the time goes in v1:
time: 626 us
  waiting for transfers between devices  561 us (90%)
  matrix products  20.9 us (3%)
  starting transfers between devices  17.4 us (3%)
  between operations  13.3 us (2%)
  other arithmetic  9.49 us (2%)
    all_gather x2, waiting for transfers between devices, apply(): column_whole = lax.all_gather(operand, 'row', axis=1, tiled=True)  406 us
    all_gather x1, waiting for transfers between devices, apply(): lax.all_gather(masked_h, 'col', axis=1, tiled=True)  77.5 us
    all_gather x1, waiting for transfers between devices, push_the_heaps(): found_now = lax.all_gather(here_x, axis_name=dev_axis)  74.1 us
    dot_general x2, matrix products, apply(): jnp.einsum('rk,skc->src', lax.all_gather(masked_h, 'col', axis=1, tiled=T...  18.6 us
  transfers between devices with their start and end apart: 8, of which 6 were waited for; matrix products, arithmetic and copies ran while one was open for 1% of the time, Pallas kernels for 0%

profile of v1, /device:TPU:1, one launch (start us, length us, event | category | flops | bytes accessed | tf_op | source)
XLA Modules:
  0.0 625.6 jit_solution(3958333334108763658)
XLA Ops:
  6.5 0.0 all-gather.12.cloned.1.call-start
  6.5 0.7 fusion.37
  7.3 4.3 collective-permute-start.1
  11.6 1.3 collective-permute-start
  12.9 0.0 collective-permute-done.1
  12.9 0.7 constant_dynamic-update-slice_fusion.1
  13.7 2.5 collective-permute-done
  16.2 3.8 collective-permute-start.2
  20.1 7.8 %collective-permute-start.3 = (f32[4,1,512]{2,1,0:T(1,128)S(1)}, f32[4,1,512]{2,1,0:T(1,128)S(1)}, u32[]{:S(2)}, u32[]{:S(2)}) collective-permute-start(f32[4,1,512]{2,1,0:T(1,128)S(1)} %get-tuple-element.9), channel_id=1, source_target_pairs={{0,1},{1,2},{2,3},{3,4},{4,5},{5,6},{6,7},{7,8},{8,9},{9,10},{10,1... | collective-permute-start | bytes 24584 | tf_op jit(solution)/shard_map/ppermute | solution.py:26
  27.9 0.0 collective-permute-done.2
  27.9 0.8 collective-permute-done.3
  28.6 0.1 select_maximum_fusion
  28.8 0.9 fusion.29
  29.7 0.0 copy-start
  29.7 2.7 multiply_convert_fusion
  32.4 0.1 copy-done
  32.5 1.7 convolution_bitcast_fusion.2
  34.2 0.0 all-gather.12.cloned.1.call-update
  34.2 0.0 all-gather.8.cloned.1.call-start
  34.3 0.8 dynamic-slice_convert_fusion.1
  35.1 0.2 mul.100
  35.2 0.0 copy-done.4
  35.2 0.8 bitcast_multiply_fusion
  36.0 0.0 all-gather.8.cloned.1.call-update
  36.0 0.0 all-gather.6.cloned.1.call-start
  36.1 0.2 mul.96
  36.3 0.0 copy-done.2
  36.3 0.9 fusion.35
  37.3 0.0 all-gather.6.cloned.1.call-update
  37.3 0.0 all-gather.10.cloned.1.call-start
  37.3 0.1 broadcast_bitcast_fusion
  37.4 74.1 %all-gather.12.cloned.1.call-done = f32[48,128,128]{2,1,0:T(8,128)} async-done(((f32[3,128,128]{2,1,0:T(8,128)}), f32[48,128,128]{2,1,0:T(8,128)}) %all-gather.12.cloned.1.call-update) | async-done | bytes 3145744 | tf_op jit(solution)/shard_map/all_gather | solution.py:13
  111.6 2.1 reduce_sum.9
  113.6 0.3 convolution_bitcast_fusion.1
  113.9 0.1 copy.24
  114.0 77.5 %all-gather.8.cloned.1.call-done = bf16[384,6144]{1,0:T(8,128)(2,1)} async-done(((bf16[384,384]{1,0:T(8,128)(2,1)}), bf16[384,6144]{1,0:T(8,128)(2,1)}) %all-gather.8.cloned.1.call-update) | async-done | bytes 4718608 | tf_op jit(solution)/shard_map/all_gather | solution.py:81
  191.5 203.1 %all-gather.6.cloned.1.call-done = bf16[2,6144,384]{2,1,0:T(8,128)(2,1)} async-done(((bf16[2,384,384]{2,1,0:T(8,128)(2,1)}), bf16[2,6144,384]{2,1,0:T(8,128)(2,1)}) %all-gather.6.cloned.1.call-update) | async-done | bytes 9437200 | tf_op jit(solution)/shard_map/all_gather | solution.py:78
  394.5 10.1 %fusion.38 = (bf16[2,384,384]{2,1,0:T(8,128)(2,1)}, f32[2,384,384]{2,1,0:T(8,128)}) fusion(f32[2,384,384]{2,1,0:T(8,128)S(1)} %bitcast.76, bf16[2,6144,384]{2,1,0:T(8,128)(2,1)} %all-gather.6.cloned.1.call-done, bf16[384,6144]{1,0:T(8,128)(2,1)} %all-gather.8.cloned.1.call-done), kind=kOutput, calls=%fused_computation.61 | convolution fusion | flops 3624468480 | bytes 17104896 | tf_op jit(solution)/shard_map/rk,skc->src/dot_general | solution.py:79
  404.7 0.0 all-gather.10.cloned.1.call-update
  404.7 0.2 mul.119
  404.9 0.1 copy.45
  404.9 0.8 copy-done.1
  405.7 0.3 convolution_bitcast_fusion
  406.0 0.1 copy.28
  406.1 203.2 %all-gather.10.cloned.1.call-done = bf16[2,6144,384]{2,1,0:T(8,128)(2,1)} async-done(((bf16[2,384,384]{2,1,0:T(8,128)(2,1)}), bf16[2,6144,384]{2,1,0:T(8,128)(2,1)}) %all-gather.10.cloned.1.call-update) | async-done | bytes 9437200 | tf_op jit(solution)/shard_map/all_gather | solution.py:78
  609.3 8.5 %fusion.13 = f32[2,384,384]{2,1,0:T(8,128)S(1)} fusion(f32[2,384,384]{2,1,0:T(8,128)S(1)} %bitcast.77, bf16[2,6144,384]{2,1,0:T(8,128)(2,1)} %all-gather.10.cloned.1.call-done, bf16[384,6144]{1,0:T(8,128)(2,1)} %all-gather.8.cloned.1.call-done), kind=kOutput, calls=%fused_computation.10 | convolution fusion | flops 3624173568 | bytes 16515072 | tf_op jit(solution)/shard_map/rk,skc->src/dot_general | solution.py:79
  617.8 0.3 fusion.19
  618.1 0.9 fusion.16
  (10 shorter events, 0.1 us)
Async XLA Ops:
  6.5 105.0 %all-gather.12.cloned.1.call-start = ((), (), s32[]{:S(2)}) async-start(), calls=%async_computation.3 | async-start | bytes 3342336 | tf_op jit(solution)/shard_map/all_gather | solution.py:13
  7.3 5.7 collective-permute-start.1
  11.6 4.6 collective-permute-start
  16.2 11.7 %collective-permute-start.2 = (f32[4,1,512]{2,1,0:T(1,128)S(1)}, f32[4,1,512]{2,1,0:T(1,128)S(1)}, u32[]{:S(2)}, u32[]{:S(2)}) collective-permute-start(f32[4,1,512]{2,1,0:T(1,128)S(1)} %get-tuple-element.10), channel_id=1, source_target_pairs={{1,0},{2,1},{3,2},{4,3},{5,4},{6,5},{7,6},{8,7},{9,8},{10,9},{11,1... | collective-permute-start | bytes 24584 | tf_op jit(solution)/shard_map/ppermute | solution.py:29
  20.1 8.6 %collective-permute-start.3 = (f32[4,1,512]{2,1,0:T(1,128)S(1)}, f32[4,1,512]{2,1,0:T(1,128)S(1)}, u32[]{:S(2)}, u32[]{:S(2)}) collective-permute-start(f32[4,1,512]{2,1,0:T(1,128)S(1)} %get-tuple-element.9), channel_id=1, source_target_pairs={{0,1},{1,2},{2,3},{3,4},{4,5},{5,6},{6,7},{7,8},{8,9},{9,10},{10,1... | collective-permute-start | bytes 24584 | tf_op jit(solution)/shard_map/ppermute | solution.py:26
  29.7 2.8 copy-start
  32.5 2.7 copy-start.4
  32.5 3.8 copy-start.2
  34.2 157.3 %all-gather.8.cloned.1.call-start = ((), (), s32[]{:S(2)}) async-start(), calls=%async_computation.1 | async-start | bytes 5013504 | tf_op jit(solution)/shard_map/all_gather | solution.py:81
  36.0 358.5 %all-gather.6.cloned.1.call-start = ((), (), s32[]{:S(2)}) async-start(), calls=%async_computation | async-start | bytes 10027008 | tf_op jit(solution)/shard_map/all_gather | solution.py:78
  37.3 572.0 %all-gather.10.cloned.1.call-start = ((), (), s32[]{:S(2)}) async-start(), calls=%async_computation.2 | async-start | bytes 10027008 | tf_op jit(solution)/shard_map/all_gather | solution.py:78
  404.7 1.1 copy-start.1
  609.3 8.5 %copy-start.3 = (f32[2,384,384]{2,1,0:T(8,128)S(1)}, f32[2,384,384]{2,1,0:T(8,128)}, u32[]{:S(2)}) copy-start(f32[2,384,384]{2,1,0:T(8,128)} %get-tuple-element.16) | copy-start | bytes 3538948
Sparse Core Ops, SparseCore 0:
  34.3 77.1 all-gather.11
  114.1 77.3 all-gather.7
  193.3 201.2 all-gather.5
  404.8 204.4 all-gather.9
